TPU v7x, 512 devices: a whole 4x4x16 slice. The times are simulated.
512 devices in a mesh: row: 32 (over z, y_lo), col: 16 (over y_hi, x, core).
Axes of the slice: x: 4, y: 4 (y_hi: 2, y_lo: 2; y = y_hi * 2 + y_lo), z: 16, core: 2. Of those that a mesh axis runs over, the one named last changes fastest.
Arguments:
- coords: int32 [3, 65536], P(None, ('row', 'col')), may hold values from 0 to 60809, as said below
- mode_shapes: bfloat16 [256, 65536], P(None, ('row', 'col')), as said below
- output_shapes: bfloat16 [1048576, 256], P(('row', 'col')), may hold values from -0.375 to 0.375
- response_gain: float32 [2, 256], replicated, may hold values from -4 to 4
Outputs:
- response_power: float32 [1048576], P(('row', 'col'))
- modal_csd: float32 [256, 256], replicated
Inputs may be any that keep to these rules, and one draw needn't show every extreme that they name: `coords`: positions of points on an aircraft's skin, numbered in no spatial order. `mode_shapes`: entries are of order 1 / sqrt(65536); each mode has a share of one sign over all nodes.
All inputs are finite; a program needn't handle non-finite values.
Results may differ from a plain program's by a relative error of at most 0.002.
Values may be sent and summed in bfloat16 or wider, within the bound.
A program may use at most 64 MiB of HBM per device.

v0:
```python
import functools
import math

import jax
import jax.numpy as jnp
from jax import lax
from jax.experimental import pallas as pl
from jax.experimental.pallas import tpu as pltpu
from jax.sharding import PartitionSpec as P

wave_scale = 0.35 / 64.0


def coherence(left_points, right_points):
    difference = left_points[:, :, None] - right_points[:, None, :]
    squared = jnp.sum(difference * difference, axis=0)
    return jnp.sinc(wave_scale * jnp.sqrt(squared)).astype(jnp.bfloat16)


def split_parts(matrix):
    high_part = matrix.astype(jnp.bfloat16)
    low_part = (matrix - high_part.astype(jnp.float32)).astype(jnp.bfloat16)
    return (high_part, low_part)


def pack_block(coords, mode_shapes):
    wide = coords.astype(jnp.float32)
    high = jnp.floor(wide * (1.0 / 256.0))
    low = wide - 256.0 * high
    pad = jnp.zeros((10, wide.shape[1]), jnp.float32)
    extra = jnp.concatenate([high, low, pad], axis=0).astype(jnp.bfloat16)
    return jnp.concatenate([mode_shapes, extra], axis=0)


def unpack_points(packed, mode_count):
    high = packed[..., mode_count:mode_count + 3, :].astype(jnp.float32)
    low = packed[..., mode_count + 3:mode_count + 6, :].astype(jnp.float32)
    return high * 256.0 + low


CHUNK = 32
SIN_TERMS = [math.pi * (-1) ** k * math.pi ** (2 * k) / math.factorial(2 * k + 1) for k in range(6)]


def coherence_chunk(dx, dy, dz):
    squared = dx * dx + dy * dy + dz * dz
    safe = jnp.maximum(squared, 1e-30)
    root_inv = lax.rsqrt(safe)
    root_inv = root_inv * (1.5 - 0.5 * safe * root_inv * root_inv)
    x = squared * root_inv * wave_scale
    n = jnp.floor(x + 0.5)
    f = x - n
    h = n * 0.5
    sign = 1.0 - 4.0 * (h - jnp.floor(h))
    f2 = f * f
    q = SIN_TERMS[5]
    for term in SIN_TERMS[4::-1]:
        q = q * f2 + term
    scale = jnp.where(n == 0.0, 1.0 / math.pi, f * root_inv * (1.0 / (math.pi * wave_scale)))
    return sign * q * scale


def block_points(slot_ref, mode_count):
    tail = slot_ref[mode_count:mode_count + 16, :].astype(jnp.float32)
    return [tail[k:k + 1, :] * 256.0 + tail[k + 3:k + 4, :] for k in range(3)]


def accumulate_block(slot_ref, weight, rowpts_ref, out_ref, tile_ref, mode_count):
    bx, by, bz = block_points(slot_ref, mode_count)
    length = tile_ref.shape[0]

    def chunk(c, carry):
        r0 = pl.multiple_of(c * CHUNK, CHUNK)
        dx = rowpts_ref[0, pl.ds(r0, CHUNK), :] - bx
        dy = rowpts_ref[1, pl.ds(r0, CHUNK), :] - by
        dz = rowpts_ref[2, pl.ds(r0, CHUNK), :] - bz
        tile_ref[pl.ds(r0, CHUNK), :] = coherence_chunk(dx, dy, dz).astype(jnp.bfloat16)
        return carry

    lax.fori_loop(0, length // CHUNK, chunk, 0)
    shapes = slot_ref[0:mode_count, :]
    product = lax.dot_general(
        tile_ref[...], shapes, (((1,), (1,)), ((), ())), preferred_element_type=jnp.float32
    )
    out_ref[...] += weight * product


def shift_of(j, rows):
    odd = j % 2
    return odd * j + (1 - odd) * (rows - j)


def row_kernel(rows, mode_count, packed_ref, rowpts_ref, out_ref, recv, tile_ref, send_sems, recv_sems):
    me = lax.axis_index("row")
    col = lax.axis_index("col")
    half = rows // 2
    barrier = pltpu.get_barrier_semaphore()
    for p in range(1, rows):
        pl.semaphore_signal(
            barrier, 1, device_id=(lax.rem(me + p, rows), col), device_id_type=pl.DeviceIdType.MESH
        )
    pl.semaphore_wait(barrier, rows - 1)

    def transfer(k):
        target = lax.rem(me + rows - shift_of(k + 1, rows), rows)
        return pltpu.make_async_remote_copy(
            src_ref=packed_ref,
            dst_ref=recv.at[k],
            send_sem=send_sems.at[k],
            recv_sem=recv_sems.at[k],
            device_id=(target, col),
            device_id_type=pl.DeviceIdType.MESH,
        )

    for k in range(half):
        transfer(k).start()
    out_ref[...] = jnp.zeros_like(out_ref)
    accumulate_block(packed_ref, 0.5, rowpts_ref, out_ref, tile_ref, mode_count)

    def step(k, carry):
        transfer(k).wait_recv()
        weight = jnp.where(k == half - 1, 0.5, 1.0).astype(jnp.float32)
        accumulate_block(recv.at[k], weight, rowpts_ref, out_ref, tile_ref, mode_count)
        return carry

    lax.fori_loop(0, half, step, 0)
    for k in range(half):
        transfer(k).wait_send()


def row_exchange(packed, rowpts, rows, mode_count):
    length = rowpts.shape[1]
    half = rows // 2
    vmem = pltpu.MemorySpace.VMEM
    flops = 2 * (half + 1) * length * packed.shape[1] * mode_count
    return pl.pallas_call(
        functools.partial(row_kernel, rows, mode_count),
        out_shape=jax.ShapeDtypeStruct((length, mode_count), jnp.float32),
        in_specs=[pl.BlockSpec(memory_space=vmem)] * 2,
        out_specs=pl.BlockSpec(memory_space=vmem),
        scratch_shapes=[
            pltpu.VMEM((half,) + packed.shape, packed.dtype),
            pltpu.VMEM((length, packed.shape[1]), jnp.bfloat16),
            pltpu.SemaphoreType.DMA((half,)),
            pltpu.SemaphoreType.DMA((half,)),
        ],
        compiler_params=pltpu.CompilerParams(
            collective_id=0, has_side_effects=True, vmem_limit_bytes=48 * 1024 * 1024
        ),
        cost_estimate=pl.CostEstimate(
            flops=flops, transcendentals=(half + 1) * length * packed.shape[1], bytes_accessed=8 * 1024 * 1024
        ),
    )(packed, rowpts)


def gather_all(block, axis, count):
    spread = jnp.broadcast_to(block[None], (count,) + block.shape)
    return lax.all_to_all(spread, axis, 0, 0, tiled=True)


def all_reduce(matrix, rows, cols):
    flat = matrix.reshape(cols, -1)
    part = lax.all_to_all(flat, "col", 0, 0, tiled=True).reshape(cols, -1).sum(0)
    part = part.reshape(rows, -1)
    part = lax.all_to_all(part, "row", 0, 0, tiled=True).reshape(rows, -1).sum(0)
    whole = gather_all(part, "row", rows).reshape(-1)
    whole = gather_all(whole, "col", cols).reshape(-1)
    return whole.reshape(matrix.shape)


def local(coords, mode_shapes, output_shapes, response_gain):
    rows = lax.axis_size("row")
    cols = lax.axis_size("col")
    mode_count, block_nodes = mode_shapes.shape
    packed = pack_block(coords, mode_shapes)
    row_packed = gather_all(packed, "col", cols)
    row_shapes = jnp.transpose(row_packed[:, :mode_count, :], (1, 0, 2)).reshape(mode_count, -1)
    row_points = jnp.transpose(unpack_points(row_packed, mode_count), (1, 0, 2)).reshape(3, -1)

    rowpts = jnp.broadcast_to(row_points[:, :, None], row_points.shape + (block_nodes,))
    projection_t = row_exchange(packed, rowpts, rows, mode_count)
    high_part, low_part = split_parts(projection_t)
    partial = jnp.dot(row_shapes, high_part, preferred_element_type=jnp.float32)
    partial = partial + jnp.dot(row_shapes, low_part, preferred_element_type=jnp.float32)
    total = all_reduce(partial, rows, cols)
    modal_csd = total + total.T
    real_part = response_gain[0]
    imag_part = response_gain[1]
    weighted = (
        real_part[:, None] * real_part[None, :] + imag_part[:, None] * imag_part[None, :]
    ) * modal_csd
    weighted_high, weighted_low = split_parts(weighted)
    mapped = jnp.dot(output_shapes, weighted_high, preferred_element_type=jnp.float32)
    mapped = mapped + jnp.dot(output_shapes, weighted_low, preferred_element_type=jnp.float32)
    response_power = jnp.sum(mapped * output_shapes.astype(jnp.float32), axis=1)
    return (response_power, modal_csd)


def solution(mesh):
    in_specs = (P(None, ("row", "col")), P(None, ("row", "col")), P(("row", "col"), None), P())
    out_specs = (P(("row", "col")), P())
    return jax.shard_map(local, mesh=mesh, in_specs=in_specs, out_specs=out_specs, check_vma=False)
```

profile of v0, /device:TPU:1, one launch (start us, length us, event | category | flops | bytes accessed | tf_op | source)
XLA Modules:
  0.0 179.9 jit_solution(9510802813695612090)
XLA Ops:
  0.6 0.7 fusion.17
  1.3 0.1 pad.3.clone
  1.4 0.9 maximum_maximum_fusion.packed_ref
  2.3 0.1 broadcast_in_dim.30
  2.5 27.7 %all_to_all.36 = bf16[16,272,128]{2,1,0:T(8,128)(2,1)S(1)} all-to-all(bf16[16,272,128]{2,1,0:T(8,128)(2,1)S(1)} %broadcast_in_dim.30), channel_id=1, replica_groups=mesh['row'=32,'col'=16] {'col'}, dimensions={0} | all-to-all | bytes 2228224 | tf_op jit(solution)/shard_map/all_to_all | solution.py:158
  30.2 0.9 broadcast_in_dim.32.rowpts_ref
  31.1 66.4 %shard_map.59 = f32[2048,256]{1,0:T(8,128)S(1)} custom-call(bf16[272,128]{1,0:T(8,128)(2,1)S(1)} %maximum_maximum_fusion.packed_ref, f32[3,2048,128]{2,1,0:T(8,128)S(1)} %broadcast_in_dim.32.rowpts_ref), custom_call_target="tpu_custom_call" | custom-call | flops 2281701376 | bytes 8388608 | tf_op jit(solution)/shard_map/pallas_call | solution.py:136
  97.5 1.1 slice.20
  98.6 1.5 copy.26
  100.1 0.5 fusion.4
  100.6 0.5 convolution_add_fusion.1
  101.0 0.0 copy-start
  101.1 0.0 copy-start.2
  101.1 0.3 all_to_all.30
  101.3 15.0 %all_to_all.37 = f32[16,1,4096]{2,1,0:T(1,128)S(1)} all-to-all(f32[16,1,4096]{2,1,0:T(1,128)S(1)} %all_to_all.30), channel_id=1, replica_groups=mesh['row'=32,'col'=16] {'col'}, dimensions={0} | all-to-all | bytes 524288 | tf_op jit(solution)/shard_map/all_to_all | solution.py:163
  116.3 0.2 reduce_sum.27
  116.5 29.1 %all_to_all.38 = f32[32,1,128]{2,1,0:T(1,128)S(1)} all-to-all(f32[32,1,128]{2,1,0:T(1,128)S(1)} %bitcast.26), channel_id=1, replica_groups=mesh['row'=32,'col'=16] {'row'}, dimensions={0} | all-to-all | bytes 32768 | tf_op jit(solution)/shard_map/all_to_all | solution.py:165
  145.7 15.0 %all_to_all.39 = f32[32,1,128]{2,1,0:T(1,128)S(1)} all-to-all(f32[32,1,128]{2,1,0:T(1,128)S(1)} %broadcast_in_dim.33), channel_id=1, replica_groups=mesh['row'=32,'col'=16] {'row'}, dimensions={0} | all-to-all | bytes 32768 | tf_op jit(solution)/shard_map/all_to_all | solution.py:158
  160.7 0.9 broadcast_in_dim.35
  161.6 6.7 %all-to-all-start.4 = ((f32[16,1,4096]{2,1,0:T(1,128)}), f32[16,1,4096]{2,1,0:T(1,128)S(1)}, u32[]{:S(2)}, u32[]{:S(2)}) async-start(f32[16,1,4096]{2,1,0:T(1,128)} %broadcast_in_dim.35), calls=%async_computation.4 | async-start | bytes 524288 | tf_op jit(solution)/shard_map/all_to_all | solution.py:158
  168.3 0.0 copy-done
  168.3 0.6 copy.25
  169.0 0.0 copy-done.2
  169.0 8.1 %all-to-all-done.4 = f32[16,1,4096]{2,1,0:T(1,128)S(1)} async-done(((f32[16,1,4096]{2,1,0:T(1,128)}), f32[16,1,4096]{2,1,0:T(1,128)S(1)}, u32[]{:S(2)}, u32[]{:S(2)}) %all-to-all-start.4) | async-done | bytes 262176 | tf_op jit(solution)/shard_map/all_to_all | solution.py:158
  177.1 0.6 reduce.2
  177.8 0.1 copy.24
  177.9 0.0 copy-start.1
  177.9 0.6 fusion.7
  178.6 1.3 fusion.2
  179.9 0.0 copy-done.1
  (7 shorter events, 0.1 us)
Async XLA Ops:
  101.0 67.3 %copy-start = (bf16[2048,256]{1,0:T(8,128)(2,1)S(1)}, bf16[2048,256]{1,0:T(8,128)(2,1)}, u32[]{:S(2)}) copy-start(bf16[2048,256]{1,0:T(8,128)(2,1)} %param.6) | copy-start | bytes 3145732
  101.1 67.9 %copy-start.2 = (f32[2,256]{1,0:T(2,128)S(1)}, f32[2,256]{1,0:T(2,128)}, u32[]{:S(2)}) copy-start(f32[2,256]{1,0:T(2,128)} %param.7) | copy-start | bytes 6148
  161.6 15.4 %all-to-all-start.4 = ((f32[16,1,4096]{2,1,0:T(1,128)}), f32[16,1,4096]{2,1,0:T(1,128)S(1)}, u32[]{:S(2)}, u32[]{:S(2)}) async-start(f32[16,1,4096]{2,1,0:T(1,128)} %broadcast_in_dim.35), calls=%async_computation.4 | async-start | bytes 524288 | tf_op jit(solution)/shard_map/all_to_all | solution.py:158
  177.9 1.9 %copy-start.1 = (f32[256,256]{1,0:T(8,128)}, f32[256,256]{1,0:T(8,128)S(1)}, u32[]{:S(2)}) copy-start(f32[256,256]{1,0:T(8,128)S(1)} %bitcast_add_fusion) | copy-start | bytes 786436
where the time goes:
time: 180 us
  blocking collectives  86.9 us (48%)
  Pallas kernels  66.4 us (37%)
  waiting for transfers between devices  8.07 us (4%)
  starting transfers between devices  6.7 us (4%)
  local copies, waits for them, and re-layouts  5.69 us (3%)
  matrix products  2.85 us (2%)
  other arithmetic  2.49 us (1%)
    pallas_call x1, Pallas kernels, row_exchange(): pl.pallas_call(functools.partial(row_kernel, rows, mode_count), out_shape...  66.4 us
    all_to_all x2, blocking collectives, gather_all(): return lax.all_to_all(spread, axis, 0, 0, tiled=True)  42.8 us
    all_to_all x1, blocking collectives, all_reduce(): lax.all_to_all(part, 'row', 0, 0, tiled=True).reshape(rows, -1).sum(0)  29.1 us
    all_to_all x1, blocking collectives, all_reduce(): lax.all_to_all(flat, 'col', 0, 0, tiled=True).reshape(cols, -1).sum(0)  15 us
    all_to_all x1, waiting for transfers between devices, gather_all(): return lax.all_to_all(spread, axis, 0, 0, tiled=True)  8.07 us
    all_to_all x1, starting transfers between devices, gather_all(): return lax.all_to_all(spread, axis, 0, 0, tiled=True)  6.7 us
  transfers between devices with their start and end apart: 1, of which 1 were waited for; matrix products, arithmetic and copies ran while one was open for 0% of the time, Pallas kernels for 0%

commit v1 on v0

--- a/solution.py
+++ b/solution.py
@@ -158,14 +158,94 @@
     return lax.all_to_all(spread, axis, 0, 0, tiled=True)
 
 
+def ar_kernel(rows, cols, y_ref, out_ref, buf_a, buf_b, buf_c, red_a, red_b, sa, ra, sb, rb, sc, rc):
+    me_r = lax.axis_index("row")
+    me_c = lax.axis_index("col")
+    buf_a[...] = jnp.zeros_like(buf_a)
+    buf_b[...] = jnp.zeros_like(buf_b)
+    buf_c[...] = jnp.zeros_like(buf_c)
+    barrier = pltpu.get_barrier_semaphore()
+    for p in range(1, cols):
+        pl.semaphore_signal(
+            barrier, 1, device_id=(me_r, lax.rem(me_c + p, cols)), device_id_type=pl.DeviceIdType.MESH
+        )
+    for p in range(1, rows):
+        pl.semaphore_signal(
+            barrier, 1, device_id=(lax.rem(me_r + p, rows), me_c), device_id_type=pl.DeviceIdType.MESH
+        )
+    pl.semaphore_wait(barrier, cols - 1 + rows - 1)
+
+    def copy(src, buf, slot, send, recv, sem_index, peer):
+        return pltpu.make_async_remote_copy(
+            src_ref=src,
+            dst_ref=buf.at[slot],
+            send_sem=send.at[sem_index],
+            recv_sem=recv.at[slot],
+            device_id=peer,
+            device_id_type=pl.DeviceIdType.MESH,
+        )
+
+    def exchange(src_of, buf, send, recv, count, me, peer_of):
+        for s in range(count):
+            @pl.when(s != me)
+            def _():
+                copy(src_of(s), buf, me, send, recv, s, peer_of(s)).start()
+        for s in range(count):
+            @pl.when(s != me)
+            def _():
+                copy(src_of(s), buf, s, send, recv, s, peer_of(s)).wait_recv()
+
+    def finish(src_of, buf, send, recv, count, me, peer_of):
+        for s in range(count):
+            @pl.when(s != me)
+            def _():
+                copy(src_of(s), buf, me, send, recv, s, peer_of(s)).wait_send()
+
+    col_peer = lambda s: (me_r, s)
+    row_peer = lambda s: (s, me_c)
+    exchange(lambda s: y_ref.at[s], buf_a, sa, ra, cols, me_c, col_peer)
+    chunk = y_ref[me_c]
+    for s in range(cols):
+        chunk = chunk + buf_a[s]
+    red_a[...] = chunk
+    exchange(lambda s: red_a, buf_b, sb, rb, rows, me_r, row_peer)
+    total = jnp.zeros_like(chunk)
+    for s in range(rows):
+        total = total + jnp.where(s == me_r, chunk, buf_b[s])
+    red_b[...] = total
+    exchange(lambda s: red_b, buf_c, sc, rc, cols, me_c, col_peer)
+    for s in range(cols):
+        out_ref[s] = jnp.where(s == me_c, total, buf_c[s])
+    finish(lambda s: y_ref.at[s], buf_a, sa, ra, cols, me_c, col_peer)
+    finish(lambda s: red_a, buf_b, sb, rb, rows, me_r, row_peer)
+    finish(lambda s: red_b, buf_c, sc, rc, cols, me_c, col_peer)
+
+
 def all_reduce(matrix, rows, cols):
-    flat = matrix.reshape(cols, -1)
-    part = lax.all_to_all(flat, "col", 0, 0, tiled=True).reshape(cols, -1).sum(0)
-    part = part.reshape(rows, -1)
-    part = lax.all_to_all(part, "row", 0, 0, tiled=True).reshape(rows, -1).sum(0)
-    whole = gather_all(part, "row", rows).reshape(-1)
-    whole = gather_all(whole, "col", cols).reshape(-1)
-    return whole.reshape(matrix.shape)
+    pieces = matrix.reshape(cols, -1, 128)
+    shape = pieces.shape
+    vmem = pltpu.MemorySpace.VMEM
+    total = pl.pallas_call(
+        functools.partial(ar_kernel, rows, cols),
+        out_shape=jax.ShapeDtypeStruct(shape, jnp.float32),
+        in_specs=[pl.BlockSpec(memory_space=vmem)],
+        out_specs=pl.BlockSpec(memory_space=vmem),
+        scratch_shapes=[
+            pltpu.VMEM(shape, jnp.float32),
+            pltpu.VMEM((rows,) + shape[1:], jnp.float32),
+            pltpu.VMEM(shape, jnp.float32),
+            pltpu.VMEM(shape[1:], jnp.float32),
+            pltpu.VMEM(shape[1:], jnp.float32),
+            pltpu.SemaphoreType.DMA((cols,)),
+            pltpu.SemaphoreType.DMA((cols,)),
+            pltpu.SemaphoreType.DMA((rows,)),
+            pltpu.SemaphoreType.DMA((rows,)),
+            pltpu.SemaphoreType.DMA((cols,)),
+            pltpu.SemaphoreType.DMA((cols,)),
+        ],
+        compiler_params=pltpu.CompilerParams(collective_id=1, has_side_effects=True),
+    )(pieces)
+    return total.reshape(matrix.shape)
 
 
 def local(coords, mode_shapes, output_shapes, response_gain):

time: 180 us -> 164 us (0.911)
  the two profiles are of different devices: /device:TPU:1 before, /device:TPU:161 now
where the time goes in v1:
time: 164 us
  Pallas kernels  126 us (77%)
  waiting for transfers between devices  16.6 us (10%)
  local copies, waits for them, and re-layouts  8.62 us (5%)
  starting transfers between devices  7.75 us (5%)
  matrix products  2.82 us (2%)
  other arithmetic  1.77 us (1%)
    pallas_call x1, Pallas kernels, row_exchange(): pl.pallas_call(functools.partial(row_kernel, rows, mode_count), out_shape...  63.3 us
    pallas_call x1, Pallas kernels, all_reduce(): pl.pallas_call(functools.partial(ar_kernel, rows, cols), out_shape=jax.Sh...  62.4 us
    all_to_all x1, waiting for transfers between devices, gather_all(): return lax.all_to_all(spread, axis, 0, 0, tiled=True)  16.6 us
    all_to_all x1, starting transfers between devices, gather_all(): return lax.all_to_all(spread, axis, 0, 0, tiled=True)  7.75 us
    unnamed x12, local copies, waits for them, and re-layouts  3.58 us
  transfers between devices with their start and end apart: 1, of which 1 were waited for; matrix products, arithmetic and copies ran while one was open for 1% of the time, Pallas kernels for 0%

profile of v1, /device:TPU:161, one launch (start us, length us, event | category | flops | bytes accessed | tf_op | source)
XLA Modules:
  0.0 164.0 jit_solution(13734890149033665668)
XLA Ops:
  0.6 0.0 copy-start
  0.6 0.8 fusion.17
  1.4 0.1 pad.3.clone
  1.5 0.9 maximum_maximum_fusion.packed_ref
  2.4 1.1 broadcast_in_dim.17
  3.6 0.0 copy-start.4
  3.6 7.7 %all-to-all-start = ((bf16[16,272,128]{2,1,0:T(8,128)(2,1)}), bf16[16,272,128]{2,1,0:T(8,128)(2,1)S(1)}, u32[]{:S(2)}, u32[]{:S(2)}) async-start(bf16[16,272,128]{2,1,0:T(8,128)(2,1)} %broadcast_in_dim.17), calls=%async_computation | async-start | bytes 2228224 | tf_op jit(solution)/shard_map/all_to_all | solution.py:158
  11.3 0.0 copy-done
  11.3 1.4 copy.12
  12.8 0.0 copy-done.4
  12.8 16.6 %all-to-all-done = bf16[16,272,128]{2,1,0:T(8,128)(2,1)S(1)} async-done(((bf16[16,272,128]{2,1,0:T(8,128)(2,1)}), bf16[16,272,128]{2,1,0:T(8,128)(2,1)S(1)}, u32[]{:S(2)}, u32[]{:S(2)}) %all-to-all-start) | async-done | bytes 1114144 | tf_op jit(solution)/shard_map/all_to_all | solution.py:158
  29.4 0.9 broadcast_in_dim.19.rowpts_ref
  30.3 63.3 %shard_map.59 = f32[2048,256]{1,0:T(8,128)S(1)} custom-call(bf16[272,128]{1,0:T(8,128)(2,1)S(1)} %maximum_maximum_fusion.packed_ref, f32[3,2048,128]{2,1,0:T(8,128)S(1)} %broadcast_in_dim.19.rowpts_ref), custom_call_target="tpu_custom_call" | custom-call | flops 2281701376 | bytes 8388608 | tf_op jit(solution)/shard_map/pallas_call | solution.py:136
  93.6 1.1 slice.20
  94.6 1.5 copy.13
  96.1 0.5 fusion.4
  96.6 0.5 convolution_add_fusion.1
  97.1 0.0 copy-start.1
  97.1 0.7 reshape.18.y_ref
  97.8 62.4 %shard_map.60 = f32[16,32,128]{2,1,0:T(8,128)} custom-call(f32[16,32,128]{2,1,0:T(8,128)} %reshape.18.y_ref), custom_call_target="tpu_custom_call" | custom-call | tf_op jit(solution)/shard_map/pallas_call | solution.py:228
  160.2 1.0 reshape.19
  161.2 0.1 copy.11
  161.4 0.0 copy-start.2
  161.4 0.0 copy-start.3
  161.4 0.0 copy-done.1
  161.4 0.6 fusion.7
  162.1 0.6 copy-done.2
  162.7 1.3 fusion.2
  164.0 0.0 copy-done.3
  (4 shorter events, 0.1 us)
Async XLA Ops:
  0.6 10.7 %copy-start = (bf16[2048,256]{1,0:T(8,128)(2,1)S(1)}, bf16[2048,256]{1,0:T(8,128)(2,1)}, u32[]{:S(2)}) copy-start(bf16[2048,256]{1,0:T(8,128)(2,1)} %param.6) | copy-start | bytes 3145732
  3.6 9.2 %copy-start.4 = (f32[2,256]{1,0:T(2,128)S(1)}, f32[2,256]{1,0:T(2,128)}, u32[]{:S(2)}) copy-start(f32[2,256]{1,0:T(2,128)} %param.7) | copy-start | bytes 6148
  3.6 25.8 %all-to-all-start = ((bf16[16,272,128]{2,1,0:T(8,128)(2,1)}), bf16[16,272,128]{2,1,0:T(8,128)(2,1)S(1)}, u32[]{:S(2)}, u32[]{:S(2)}) async-start(bf16[16,272,128]{2,1,0:T(8,128)(2,1)} %broadcast_in_dim.17), calls=%async_computation | async-start | bytes 2228224 | tf_op jit(solution)/shard_map/all_to_all | solution.py:158
  97.1 64.3 %copy-start.1 = (bf16[2048,256]{1,0:T(8,128)(2,1)S(1)}, bf16[2048,256]{1,0:T(8,128)(2,1)}, u32[]{:S(2)}) copy-start(bf16[2048,256]{1,0:T(8,128)(2,1)} %param.6) | copy-start | bytes 3145732
  161.4 1.3 copy-start.2
  161.4 2.5 %copy-start.3 = (f32[256,256]{1,0:T(8,128)}, f32[256,256]{1,0:T(8,128)S(1)}, u32[]{:S(2)}) copy-start(f32[256,256]{1,0:T(8,128)S(1)} %bitcast_add_fusion) | copy-start | bytes 786436

commit v2 on v1

--- a/solution.py
+++ b/solution.py
@@ -90,16 +90,33 @@
     return odd * j + (1 - odd) * (rows - j)
 
 
-def row_kernel(rows, mode_count, packed_ref, rowpts_ref, out_ref, recv, tile_ref, send_sems, recv_sems):
+def row_kernel(rows, cols, mode_count, packed_ref, out_ref, recv, colbuf, rowpts_ref, tile_ref, acc_ref,
+               send_sems, recv_sems, col_send, col_recv):
     me = lax.axis_index("row")
     col = lax.axis_index("col")
     half = rows // 2
+    nodes = packed_ref.shape[1]
+    colbuf[...] = jnp.zeros_like(colbuf)
     barrier = pltpu.get_barrier_semaphore()
     for p in range(1, rows):
         pl.semaphore_signal(
             barrier, 1, device_id=(lax.rem(me + p, rows), col), device_id_type=pl.DeviceIdType.MESH
         )
-    pl.semaphore_wait(barrier, rows - 1)
+    for p in range(1, cols):
+        pl.semaphore_signal(
+            barrier, 1, device_id=(me, lax.rem(col + p, cols)), device_id_type=pl.DeviceIdType.MESH
+        )
+    pl.semaphore_wait(barrier, rows - 1 + cols - 1)
+
+    def col_copy(s, slot):
+        return pltpu.make_async_remote_copy(
+            src_ref=packed_ref,
+            dst_ref=colbuf.at[slot],
+            send_sem=col_send.at[s],
+            recv_sem=col_recv.at[slot],
+            device_id=(me, s),
+            device_id_type=pl.DeviceIdType.MESH,
+        )
 
     def transfer(k):
         target = lax.rem(me + rows - shift_of(k + 1, rows), rows)
@@ -112,46 +129,86 @@
             device_id_type=pl.DeviceIdType.MESH,
         )
 
+    for s in range(cols):
+        @pl.when(s != col)
+        def _():
+            col_copy(s, col).start()
     for k in range(half):
         transfer(k).start()
-    out_ref[...] = jnp.zeros_like(out_ref)
-    accumulate_block(packed_ref, 0.5, rowpts_ref, out_ref, tile_ref, mode_count)
+    for s in range(cols):
+        @pl.when(s != col)
+        def _():
+            col_copy(s, s).wait_recv()
+
+    eye = (lax.broadcasted_iota(jnp.int32, (nodes, nodes), 0)
+           == lax.broadcasted_iota(jnp.int32, (nodes, nodes), 1)).astype(jnp.bfloat16)
+    own_tail = packed_ref[mode_count:mode_count + 16, :]
+    for s in range(cols):
+        tail = jnp.where(s == col, own_tail, colbuf[s, mode_count:mode_count + 16, :])
+        moved = lax.dot_general(eye, tail, (((1,), (1,)), ((), ())), preferred_element_type=jnp.float32)
+        for k in range(3):
+            column = moved[:, k:k + 1] * 256.0 + moved[:, k + 3:k + 4]
+            rowpts_ref[k, s * nodes:(s + 1) * nodes, :] = jnp.broadcast_to(column, (nodes, nodes))
+
+    acc_ref[...] = jnp.zeros_like(acc_ref)
+    accumulate_block(packed_ref, 0.5, rowpts_ref, acc_ref, tile_ref, mode_count)
 
     def step(k, carry):
         transfer(k).wait_recv()
         weight = jnp.where(k == half - 1, 0.5, 1.0).astype(jnp.float32)
-        accumulate_block(recv.at[k], weight, rowpts_ref, out_ref, tile_ref, mode_count)
+        accumulate_block(recv.at[k], weight, rowpts_ref, acc_ref, tile_ref, mode_count)
         return carry
 
     lax.fori_loop(0, half, step, 0)
+
+    own_shapes = packed_ref[0:mode_count, :]
+    partial = jnp.zeros(out_ref.shape, jnp.float32)
+    for s in range(cols):
+        shapes = jnp.where(s == col, own_shapes, colbuf[s, 0:mode_count, :])
+        part = acc_ref[s * nodes:(s + 1) * nodes, :]
+        high = part.astype(jnp.bfloat16)
+        low = (part - high.astype(jnp.float32)).astype(jnp.bfloat16)
+        partial = partial + jnp.dot(shapes, high, preferred_element_type=jnp.float32)
+        partial = partial + jnp.dot(shapes, low, preferred_element_type=jnp.float32)
+    out_ref[...] = partial
+
     for k in range(half):
         transfer(k).wait_send()
-
-
-def row_exchange(packed, rowpts, rows, mode_count):
-    length = rowpts.shape[1]
+    for s in range(cols):
+        @pl.when(s != col)
+        def _():
+            col_copy(s, col).wait_send()
+
+
+def row_exchange(packed, rows, cols, mode_count):
+    nodes = packed.shape[1]
+    length = cols * nodes
     half = rows // 2
     vmem = pltpu.MemorySpace.VMEM
-    flops = 2 * (half + 1) * length * packed.shape[1] * mode_count
+    flops = 2 * (half + 1) * length * nodes * mode_count + 4 * length * mode_count * mode_count
     return pl.pallas_call(
-        functools.partial(row_kernel, rows, mode_count),
-        out_shape=jax.ShapeDtypeStruct((length, mode_count), jnp.float32),
-        in_specs=[pl.BlockSpec(memory_space=vmem)] * 2,
+        functools.partial(row_kernel, rows, cols, mode_count),
+        out_shape=jax.ShapeDtypeStruct((mode_count, mode_count), jnp.float32),
+        in_specs=[pl.BlockSpec(memory_space=vmem)],
         out_specs=pl.BlockSpec(memory_space=vmem),
         scratch_shapes=[
             pltpu.VMEM((half,) + packed.shape, packed.dtype),
-            pltpu.VMEM((length, packed.shape[1]), jnp.bfloat16),
+            pltpu.VMEM((cols,) + packed.shape, packed.dtype),
+            pltpu.VMEM((3, length, nodes), jnp.float32),
+            pltpu.VMEM((length, nodes), jnp.bfloat16),
+            pltpu.VMEM((length, mode_count), jnp.float32),
             pltpu.SemaphoreType.DMA((half,)),
             pltpu.SemaphoreType.DMA((half,)),
+            pltpu.SemaphoreType.DMA((cols,)),
+            pltpu.SemaphoreType.DMA((cols,)),
         ],
         compiler_params=pltpu.CompilerParams(
             collective_id=0, has_side_effects=True, vmem_limit_bytes=48 * 1024 * 1024
         ),
         cost_estimate=pl.CostEstimate(
-            flops=flops, transcendentals=(half + 1) * length * packed.shape[1], bytes_accessed=8 * 1024 * 1024
+            flops=flops, transcendentals=(half + 1) * length * nodes, bytes_accessed=4 * 1024 * 1024
         ),
-    )(packed, rowpts)
-
+    )(packed)
 
 def gather_all(block, axis, count):
     spread = jnp.broadcast_to(block[None], (count,) + block.shape)
@@ -253,15 +310,7 @@
     cols = lax.axis_size("col")
     mode_count, block_nodes = mode_shapes.shape
     packed = pack_block(coords, mode_shapes)
-    row_packed = gather_all(packed, "col", cols)
-    row_shapes = jnp.transpose(row_packed[:, :mode_count, :], (1, 0, 2)).reshape(mode_count, -1)
-    row_points = jnp.transpose(unpack_points(row_packed, mode_count), (1, 0, 2)).reshape(3, -1)
-
-    rowpts = jnp.broadcast_to(row_points[:, :, None], row_points.shape + (block_nodes,))
-    projection_t = row_exchange(packed, rowpts, rows, mode_count)
-    high_part, low_part = split_parts(projection_t)
-    partial = jnp.dot(row_shapes, high_part, preferred_element_type=jnp.float32)
-    partial = partial + jnp.dot(row_shapes, low_part, preferred_element_type=jnp.float32)
+    partial = row_exchange(packed, rows, cols, mode_count)
     total = all_reduce(partial, rows, cols)
     modal_csd = total + total.T
     real_part = response_gain[0]

time: 164 us -> 151 us (0.921)
  the two profiles are of different devices: /device:TPU:161 before, /device:TPU:505 now
where the time goes in v2:
time: 151 us
  Pallas kernels  143 us (95%)
  local copies, waits for them, and re-layouts  3.38 us (2%)
  matrix products  1.88 us (1%)
  other arithmetic  1.66 us (1%)
    pallas_call x1, Pallas kernels, row_exchange(): pl.pallas_call(functools.partial(row_kernel, rows, cols, mode_count), out...  82.4 us
    pallas_call x1, Pallas kernels, all_reduce(): pl.pallas_call(functools.partial(ar_kernel, rows, cols), out_shape=jax.Sh...  60.6 us

profile of v2, /device:TPU:505, one launch (start us, length us, event | category | flops | bytes accessed | tf_op | source)
XLA Modules:
  0.0 150.7 jit_solution(11162079336993280001)
XLA Ops:
  0.6 0.1 pad.3.clone
  0.7 0.7 fusion.14
  1.4 0.8 fusion.15
  2.2 0.9 maximum_maximum_fusion.packed_ref
  3.1 82.4 %shard_map.59 = f32[256,256]{1,0:T(8,128)S(1)} custom-call(bf16[272,128]{1,0:T(8,128)(2,1)S(1)} %maximum_maximum_fusion.packed_ref), custom_call_target="tpu_custom_call" | custom-call | flops 2818572288 | bytes 4194304 | tf_op jit(solution)/shard_map/pallas_call | solution.py:189
  85.5 0.0 copy-start
  85.5 0.7 reshape.12.y_ref
  86.2 60.6 %shard_map.60 = f32[16,32,128]{2,1,0:T(8,128)} custom-call(f32[16,32,128]{2,1,0:T(8,128)} %reshape.12.y_ref), custom_call_target="tpu_custom_call" | custom-call | tf_op jit(solution)/shard_map/pallas_call | solution.py:285
  146.9 1.0 reshape.13
  147.9 0.1 copy.6
  148.1 0.0 copy-done
  148.1 0.0 copy-start.1
  148.1 0.6 copy.7
  148.8 0.6 fusion.4
  149.4 0.0 copy-done.1
  149.4 1.3 fusion.2
  (2 shorter events, 0.0 us)
Async XLA Ops:
  85.5 62.6 %copy-start = (bf16[2048,256]{1,0:T(8,128)(2,1)S(1)}, bf16[2048,256]{1,0:T(8,128)(2,1)}, u32[]{:S(2)}) copy-start(bf16[2048,256]{1,0:T(8,128)(2,1)} %param.6) | copy-start | bytes 3145732
  148.1 1.3 copy-start.1

commit v3 on v2

--- a/solution.py
+++ b/solution.py
@@ -46,17 +46,16 @@
     squared = dx * dx + dy * dy + dz * dz
     safe = jnp.maximum(squared, 1e-30)
     root_inv = lax.rsqrt(safe)
-    root_inv = root_inv * (1.5 - 0.5 * safe * root_inv * root_inv)
-    x = squared * root_inv * wave_scale
+    x = safe * root_inv * wave_scale
     n = jnp.floor(x + 0.5)
     f = x - n
     h = n * 0.5
     sign = 1.0 - 4.0 * (h - jnp.floor(h))
     f2 = f * f
-    q = SIN_TERMS[5]
-    for term in SIN_TERMS[4::-1]:
+    q = SIN_TERMS[4]
+    for term in SIN_TERMS[3::-1]:
         q = q * f2 + term
-    scale = jnp.where(n == 0.0, 1.0 / math.pi, f * root_inv * (1.0 / (math.pi * wave_scale)))
+    scale = f * root_inv * (1.0 / (math.pi * wave_scale))
     return sign * q * scale
 
 

time: 151 us -> 147 us (0.974)
  Pallas kernels: 143 us -> 140 us
    pallas_call x1, Pallas kernels: 82.4 us -> 74.9 us  [row_exchange(): pl.pallas_call(functools.partial(row_kernel, rows, cols, mode_count), out...]
    pallas_call x1, Pallas kernels: 60.6 us -> 64.6 us  [all_reduce(): pl.pallas_call(functools.partial(ar_kernel, rows, cols), out_shape=jax.Sh...]
where the time goes in v3:
time: 147 us
  Pallas kernels  140 us (95%)
  local copies, waits for them, and re-layouts  3.38 us (2%)
  matrix products  1.89 us (1%)
  other arithmetic  1.66 us (1%)
    pallas_call x1, Pallas kernels, row_exchange(): pl.pallas_call(functools.partial(row_kernel, rows, cols, mode_count), out...  74.9 us
    pallas_call x1, Pallas kernels, all_reduce(): pl.pallas_call(functools.partial(ar_kernel, rows, cols), out_shape=jax.Sh...  64.6 us

profile of v3, /device:TPU:505, one launch (start us, length us, event | category | flops | bytes accessed | tf_op | source)
XLA Modules:
  0.0 147.2 jit_solution(1439536693453751757)
XLA Ops:
  0.6 0.1 pad.3.clone
  0.7 0.7 fusion.14
  1.4 0.8 fusion.15
  2.2 0.9 maximum_maximum_fusion.packed_ref
  3.1 74.9 %shard_map.59 = f32[256,256]{1,0:T(8,128)S(1)} custom-call(bf16[272,128]{1,0:T(8,128)(2,1)S(1)} %maximum_maximum_fusion.packed_ref), custom_call_target="tpu_custom_call" | custom-call | flops 2818572288 | bytes 4194304 | tf_op jit(solution)/shard_map/pallas_call | solution.py:188
  78.1 0.0 copy-start
  78.1 0.7 reshape.12.y_ref
  78.8 64.6 %shard_map.60 = f32[16,32,128]{2,1,0:T(8,128)} custom-call(f32[16,32,128]{2,1,0:T(8,128)} %reshape.12.y_ref), custom_call_target="tpu_custom_call" | custom-call | tf_op jit(solution)/shard_map/pallas_call | solution.py:284
  143.4 1.0 reshape.13
  144.4 0.1 copy.6
  144.6 0.0 copy-done
  144.6 0.0 copy-start.1
  144.6 0.6 copy.7
  145.3 0.6 fusion.4
  145.9 0.0 copy-done.1
  145.9 1.3 fusion.2
  (2 shorter events, 0.0 us)
Async XLA Ops:
  78.1 66.5 %copy-start = (bf16[2048,256]{1,0:T(8,128)(2,1)S(1)}, bf16[2048,256]{1,0:T(8,128)(2,1)}, u32[]{:S(2)}) copy-start(bf16[2048,256]{1,0:T(8,128)(2,1)} %param.6) | copy-start | bytes 3145732
  144.6 1.3 copy-start.1

commit v4 on v3

--- a/solution.py
+++ b/solution.py
@@ -214,11 +214,13 @@
     return lax.all_to_all(spread, axis, 0, 0, tiled=True)
 
 
-def ar_kernel(rows, cols, y_ref, out_ref, buf_a, buf_b, buf_c, red_a, red_b, sa, ra, sb, rb, sc, rc):
+def ar_kernel(rows, cols, y_ref, out_ref, buf_a, buf_b, buf_g, buf_c, red_a, red_b, red_c,
+              sa, ra, sb, rb, sg, rg, sc, rc):
     me_r = lax.axis_index("row")
     me_c = lax.axis_index("col")
     buf_a[...] = jnp.zeros_like(buf_a)
     buf_b[...] = jnp.zeros_like(buf_b)
+    buf_g[...] = jnp.zeros_like(buf_g)
     buf_c[...] = jnp.zeros_like(buf_c)
     barrier = pltpu.get_barrier_semaphore()
     for p in range(1, cols):
@@ -231,54 +233,61 @@
         )
     pl.semaphore_wait(barrier, cols - 1 + rows - 1)
 
-    def copy(src, buf, slot, send, recv, sem_index, peer):
+    def copy(src, dst, send, recv, sem_index, slot, peer):
         return pltpu.make_async_remote_copy(
             src_ref=src,
-            dst_ref=buf.at[slot],
+            dst_ref=dst,
             send_sem=send.at[sem_index],
             recv_sem=recv.at[slot],
             device_id=peer,
             device_id_type=pl.DeviceIdType.MESH,
         )
 
-    def exchange(src_of, buf, send, recv, count, me, peer_of):
+    def exchange(src_of, dst_of, send, recv, count, me, peer_of):
         for s in range(count):
             @pl.when(s != me)
             def _():
-                copy(src_of(s), buf, me, send, recv, s, peer_of(s)).start()
+                copy(src_of(s), dst_of(me), send, recv, s, me, peer_of(s)).start()
         for s in range(count):
             @pl.when(s != me)
             def _():
-                copy(src_of(s), buf, s, send, recv, s, peer_of(s)).wait_recv()
-
-    def finish(src_of, buf, send, recv, count, me, peer_of):
+                copy(src_of(s), dst_of(s), send, recv, s, s, peer_of(s)).wait_recv()
+
+    def finish(src_of, dst_of, send, recv, count, me, peer_of):
         for s in range(count):
             @pl.when(s != me)
             def _():
-                copy(src_of(s), buf, me, send, recv, s, peer_of(s)).wait_send()
+                copy(src_of(s), dst_of(me), send, recv, s, me, peer_of(s)).wait_send()
 
     col_peer = lambda s: (me_r, s)
     row_peer = lambda s: (s, me_c)
-    exchange(lambda s: y_ref.at[s], buf_a, sa, ra, cols, me_c, col_peer)
+    col_a = (lambda s: y_ref.at[s], lambda s: buf_a.at[s], sa, ra, cols, me_c, col_peer)
+    exchange(*col_a)
     chunk = y_ref[me_c]
     for s in range(cols):
         chunk = chunk + buf_a[s]
     red_a[...] = chunk
-    exchange(lambda s: red_a, buf_b, sb, rb, rows, me_r, row_peer)
-    total = jnp.zeros_like(chunk)
-    for s in range(rows):
-        total = total + jnp.where(s == me_r, chunk, buf_b[s])
-    red_b[...] = total
-    exchange(lambda s: red_b, buf_c, sc, rc, cols, me_c, col_peer)
+    row_b = (lambda s: red_a.at[pl.ds(s, 1)], lambda s: buf_b.at[pl.ds(s, 1)], sb, rb, rows, me_r, row_peer)
+    exchange(*row_b)
+    piece = red_a[pl.ds(me_r, 1), :] + jnp.sum(buf_b[...], axis=0, keepdims=True)
+    red_b[...] = piece
+    row_g = (lambda s: red_b, lambda s: buf_g.at[pl.ds(s, 1)], sg, rg, rows, me_r, row_peer)
+    exchange(*row_g)
+    lines = lax.broadcasted_iota(jnp.int32, chunk.shape, 0)
+    total = jnp.where(lines == me_r, jnp.broadcast_to(piece, chunk.shape), buf_g[...])
+    red_c[...] = total
+    col_c = (lambda s: red_c, lambda s: buf_c.at[s], sc, rc, cols, me_c, col_peer)
+    exchange(*col_c)
     for s in range(cols):
         out_ref[s] = jnp.where(s == me_c, total, buf_c[s])
-    finish(lambda s: y_ref.at[s], buf_a, sa, ra, cols, me_c, col_peer)
-    finish(lambda s: red_a, buf_b, sb, rb, rows, me_r, row_peer)
-    finish(lambda s: red_b, buf_c, sc, rc, cols, me_c, col_peer)
+    finish(*col_a)
+    finish(*row_b)
+    finish(*row_g)
+    finish(*col_c)
 
 
 def all_reduce(matrix, rows, cols):
-    pieces = matrix.reshape(cols, -1, 128)
+    pieces = matrix.reshape(cols, rows, -1)
     shape = pieces.shape
     vmem = pltpu.MemorySpace.VMEM
     total = pl.pallas_call(
@@ -288,12 +297,16 @@
         out_specs=pl.BlockSpec(memory_space=vmem),
         scratch_shapes=[
             pltpu.VMEM(shape, jnp.float32),
-            pltpu.VMEM((rows,) + shape[1:], jnp.float32),
+            pltpu.VMEM(shape[1:], jnp.float32),
+            pltpu.VMEM(shape[1:], jnp.float32),
             pltpu.VMEM(shape, jnp.float32),
             pltpu.VMEM(shape[1:], jnp.float32),
+            pltpu.VMEM((1, shape[2]), jnp.float32),
             pltpu.VMEM(shape[1:], jnp.float32),
             pltpu.SemaphoreType.DMA((cols,)),
             pltpu.SemaphoreType.DMA((cols,)),
+            pltpu.SemaphoreType.DMA((rows,)),
+            pltpu.SemaphoreType.DMA((rows,)),
             pltpu.SemaphoreType.DMA((rows,)),
             pltpu.SemaphoreType.DMA((rows,)),
             pltpu.SemaphoreType.DMA((cols,)),
@@ -302,7 +315,6 @@
         compiler_params=pltpu.CompilerParams(collective_id=1, has_side_effects=True),
     )(pieces)
     return total.reshape(matrix.shape)
-
 
 def local(coords, mode_shapes, output_shapes, response_gain):
     rows = lax.axis_size("row")

time: 147 us -> 142 us (0.966)
  the two profiles are of different devices: /device:TPU:505 before, /device:TPU:1 now
where the time goes in v4:
time: 142 us; the launch traced here: 141 us
  Pallas kernels  134 us (94%)
  local copies, waits for them, and re-layouts  3.38 us (2%)
  matrix products  1.89 us (1%)
  other arithmetic  1.66 us (1%)
    pallas_call x1, Pallas kernels, row_exchange(): pl.pallas_call(functools.partial(row_kernel, rows, cols, mode_count), out...  85.1 us
    pallas_call x1, Pallas kernels, all_reduce(): pl.pallas_call(functools.partial(ar_kernel, rows, cols), out_shape=jax.Sh...  48.6 us

profile of v4, /device:TPU:1, one launch (start us, length us, event | category | flops | bytes accessed | tf_op | source)
XLA Modules:
  0.0 141.4 jit_solution(13567901279585969047)
XLA Ops:
  0.6 0.1 pad.3.clone
  0.7 0.7 fusion.14
  1.4 0.8 fusion.15
  2.2 0.9 maximum_maximum_fusion.packed_ref
  3.1 85.1 %shard_map.59 = f32[256,256]{1,0:T(8,128)S(1)} custom-call(bf16[272,128]{1,0:T(8,128)(2,1)S(1)} %maximum_maximum_fusion.packed_ref), custom_call_target="tpu_custom_call" | custom-call | flops 2818572288 | bytes 4194304 | tf_op jit(solution)/shard_map/pallas_call | solution.py:188
  88.3 0.0 copy-start
  88.3 0.7 reshape.12.y_ref
  89.0 48.6 %shard_map.60 = f32[16,32,128]{2,1,0:T(8,128)} custom-call(f32[16,32,128]{2,1,0:T(8,128)} %reshape.12.y_ref), custom_call_target="tpu_custom_call" | custom-call | tf_op jit(solution)/shard_map/pallas_call | solution.py:293
  137.6 1.0 reshape.13
  138.6 0.1 copy.6
  138.8 0.0 copy-done
  138.8 0.0 copy-start.1
  138.8 0.6 copy.7
  139.5 0.6 fusion.4
  140.1 0.0 copy-done.1
  140.1 1.3 fusion.2
  (2 shorter events, 0.0 us)
Async XLA Ops:
  88.3 50.6 %copy-start = (bf16[2048,256]{1,0:T(8,128)(2,1)S(1)}, bf16[2048,256]{1,0:T(8,128)(2,1)}, u32[]{:S(2)}) copy-start(bf16[2048,256]{1,0:T(8,128)(2,1)} %param.6) | copy-start | bytes 3145732
  138.8 1.3 copy-start.1

commit v5 on v4

--- a/solution.py
+++ b/solution.py
@@ -76,7 +76,7 @@
         tile_ref[pl.ds(r0, CHUNK), :] = coherence_chunk(dx, dy, dz).astype(jnp.bfloat16)
         return carry
 
-    lax.fori_loop(0, length // CHUNK, chunk, 0)
+    lax.fori_loop(0, length // CHUNK, chunk, 0, unroll=2)
     shapes = slot_ref[0:mode_count, :]
     product = lax.dot_general(
         tile_ref[...], shapes, (((1,), (1,)), ((), ())), preferred_element_type=jnp.float32

time: 142 us -> 137 us (0.965)
  Pallas kernels: 134 us -> 129 us
    pallas_call x1, Pallas kernels: 85.1 us -> 78.4 us  [row_exchange(): pl.pallas_call(functools.partial(row_kernel, rows, cols, mode_count), out...]
    pallas_call x1, Pallas kernels: 48.6 us -> 50.5 us  [all_reduce(): pl.pallas_call(functools.partial(ar_kernel, rows, cols), out_shape=jax.Sh...]
where the time goes in v5:
time: 137 us
  Pallas kernels  129 us (94%)
  local copies, waits for them, and re-layouts  3.38 us (2%)
  matrix products  1.89 us (1%)
  other arithmetic  1.66 us (1%)
    pallas_call x1, Pallas kernels, row_exchange(): pl.pallas_call(functools.partial(row_kernel, rows, cols, mode_count), out...  78.4 us
    pallas_call x1, Pallas kernels, all_reduce(): pl.pallas_call(functools.partial(ar_kernel, rows, cols), out_shape=jax.Sh...  50.5 us

profile of v5, /device:TPU:1, one launch (start us, length us, event | category | flops | bytes accessed | tf_op | source)
XLA Modules:
  0.0 136.6 jit_solution(9836746584084498767)
XLA Ops:
  0.6 0.1 pad.3.clone
  0.7 0.7 fusion.14
  1.4 0.8 fusion.15
  2.2 0.9 maximum_maximum_fusion.packed_ref
  3.1 78.4 %shard_map.59 = f32[256,256]{1,0:T(8,128)S(1)} custom-call(bf16[272,128]{1,0:T(8,128)(2,1)S(1)} %maximum_maximum_fusion.packed_ref), custom_call_target="tpu_custom_call" | custom-call | flops 2818572288 | bytes 4194304 | tf_op jit(solution)/shard_map/pallas_call | solution.py:188
  81.6 0.0 copy-start
  81.6 0.7 reshape.12.y_ref
  82.3 50.5 %shard_map.60 = f32[16,32,128]{2,1,0:T(8,128)} custom-call(f32[16,32,128]{2,1,0:T(8,128)} %reshape.12.y_ref), custom_call_target="tpu_custom_call" | custom-call | tf_op jit(solution)/shard_map/pallas_call | solution.py:293
  132.8 1.0 reshape.13
  133.8 0.1 copy.6
  134.0 0.0 copy-done
  134.0 0.0 copy-start.1
  134.0 0.6 copy.7
  134.7 0.6 fusion.4
  135.3 0.0 copy-done.1
  135.3 1.3 fusion.2
  (2 shorter events, 0.0 us)
Async XLA Ops:
  81.6 52.5 %copy-start = (bf16[2048,256]{1,0:T(8,128)(2,1)S(1)}, bf16[2048,256]{1,0:T(8,128)(2,1)}, u32[]{:S(2)}) copy-start(bf16[2048,256]{1,0:T(8,128)(2,1)} %param.6) | copy-start | bytes 3145732
  134.0 1.3 copy-start.1

commit v6 on v5

--- a/solution.py
+++ b/solution.py
@@ -76,7 +76,7 @@
         tile_ref[pl.ds(r0, CHUNK), :] = coherence_chunk(dx, dy, dz).astype(jnp.bfloat16)
         return carry
 
-    lax.fori_loop(0, length // CHUNK, chunk, 0, unroll=2)
+    lax.fori_loop(0, length // CHUNK, chunk, 0, unroll=4)
     shapes = slot_ref[0:mode_count, :]
     product = lax.dot_general(
         tile_ref[...], shapes, (((1,), (1,)), ((), ())), preferred_element_type=jnp.float32

time: 137 us -> 135 us (0.985)
  Pallas kernels: 129 us -> 127 us
    pallas_call x1, Pallas kernels: 50.5 us -> 49.1 us  [all_reduce(): pl.pallas_call(functools.partial(ar_kernel, rows, cols), out_shape=jax.Sh...]
where the time goes in v6:
time: 135 us
  Pallas kernels  127 us (94%)
  local copies, waits for them, and re-layouts  3.38 us (3%)
  matrix products  1.89 us (1%)
  other arithmetic  1.66 us (1%)
    pallas_call x1, Pallas kernels, row_exchange(): pl.pallas_call(functools.partial(row_kernel, rows, cols, mode_count), out...  78.3 us
    pallas_call x1, Pallas kernels, all_reduce(): pl.pallas_call(functools.partial(ar_kernel, rows, cols), out_shape=jax.Sh...  49.1 us

profile of v6, /device:TPU:1, one launch (start us, length us, event | category | flops | bytes accessed | tf_op | source)
XLA Modules:
  0.0 135.0 jit_solution(4901395950991140500)
XLA Ops:
  0.6 0.1 pad.3.clone
  0.7 0.7 fusion.14
  1.4 0.8 fusion.15
  2.2 0.9 maximum_maximum_fusion.packed_ref
  3.1 78.3 %shard_map.59 = f32[256,256]{1,0:T(8,128)S(1)} custom-call(bf16[272,128]{1,0:T(8,128)(2,1)S(1)} %maximum_maximum_fusion.packed_ref), custom_call_target="tpu_custom_call" | custom-call | flops 2818572288 | bytes 4194304 | tf_op jit(solution)/shard_map/pallas_call | solution.py:188
  81.4 0.0 copy-start
  81.4 0.7 reshape.12.y_ref
  82.1 49.1 %shard_map.60 = f32[16,32,128]{2,1,0:T(8,128)} custom-call(f32[16,32,128]{2,1,0:T(8,128)} %reshape.12.y_ref), custom_call_target="tpu_custom_call" | custom-call | tf_op jit(solution)/shard_map/pallas_call | solution.py:293
  131.2 1.0 reshape.13
  132.3 0.1 copy.6
  132.5 0.0 copy-done
  132.5 0.0 copy-start.1
  132.5 0.6 copy.7
  133.1 0.6 fusion.4
  133.7 0.0 copy-done.1
  133.7 1.3 fusion.2
  (2 shorter events, 0.0 us)
Async XLA Ops:
  81.4 51.1 %copy-start = (bf16[2048,256]{1,0:T(8,128)(2,1)S(1)}, bf16[2048,256]{1,0:T(8,128)(2,1)}, u32[]{:S(2)}) copy-start(bf16[2048,256]{1,0:T(8,128)(2,1)} %param.6) | copy-start | bytes 3145732
  132.5 1.3 copy-start.1

commit v7 on v6

--- a/solution.py
+++ b/solution.py
@@ -76,7 +76,7 @@
         tile_ref[pl.ds(r0, CHUNK), :] = coherence_chunk(dx, dy, dz).astype(jnp.bfloat16)
         return carry
 
-    lax.fori_loop(0, length // CHUNK, chunk, 0, unroll=4)
+    lax.fori_loop(0, length // CHUNK, chunk, 0, unroll=8)
     shapes = slot_ref[0:mode_count, :]
     product = lax.dot_general(
         tile_ref[...], shapes, (((1,), (1,)), ((), ())), preferred_element_type=jnp.float32

time: 135 us -> 134 us (level)
  no operation moved by 1% of the time
where the time goes in v7:
time: 134 us
  Pallas kernels  126 us (94%)
  local copies, waits for them, and re-layouts  3.38 us (3%)
  matrix products  1.89 us (1%)
  other arithmetic  1.66 us (1%)
    pallas_call x1, Pallas kernels, row_exchange(): pl.pallas_call(functools.partial(row_kernel, rows, cols, mode_count), out...  78.1 us
    pallas_call x1, Pallas kernels, all_reduce(): pl.pallas_call(functools.partial(ar_kernel, rows, cols), out_shape=jax.Sh...  48.3 us

profile of v7, /device:TPU:1, one launch (start us, length us, event | category | flops | bytes accessed | tf_op | source)
XLA Modules:
  0.0 134.1 jit_solution(8010893340260742081)
XLA Ops:
  0.6 0.1 pad.3.clone
  0.7 0.7 fusion.14
  1.4 0.8 fusion.15
  2.2 0.9 maximum_maximum_fusion.packed_ref
  3.1 78.1 %shard_map.59 = f32[256,256]{1,0:T(8,128)S(1)} custom-call(bf16[272,128]{1,0:T(8,128)(2,1)S(1)} %maximum_maximum_fusion.packed_ref), custom_call_target="tpu_custom_call" | custom-call | flops 2818572288 | bytes 4194304 | tf_op jit(solution)/shard_map/pallas_call | solution.py:188
  81.2 0.0 copy-start
  81.3 0.7 reshape.12.y_ref
  82.0 48.3 %shard_map.60 = f32[16,32,128]{2,1,0:T(8,128)} custom-call(f32[16,32,128]{2,1,0:T(8,128)} %reshape.12.y_ref), custom_call_target="tpu_custom_call" | custom-call | tf_op jit(solution)/shard_map/pallas_call | solution.py:293
  130.3 1.0 reshape.13
  131.3 0.1 copy.6
  131.5 0.0 copy-done
  131.5 0.0 copy-start.1
  131.5 0.6 copy.7
  132.2 0.6 fusion.4
  132.8 0.0 copy-done.1
  132.8 1.3 fusion.2
  (2 shorter events, 0.0 us)
Async XLA Ops:
  81.2 50.2 %copy-start = (bf16[2048,256]{1,0:T(8,128)(2,1)S(1)}, bf16[2048,256]{1,0:T(8,128)(2,1)}, u32[]{:S(2)}) copy-start(bf16[2048,256]{1,0:T(8,128)(2,1)} %param.6) | copy-start | bytes 3145732
  131.5 1.3 copy-start.1

commit v8 on v7

--- a/solution.py
+++ b/solution.py
@@ -39,7 +39,7 @@
 
 
 CHUNK = 32
-SIN_TERMS = [math.pi * (-1) ** k * math.pi ** (2 * k) / math.factorial(2 * k + 1) for k in range(6)]
+SIN_TERMS = [(-1) ** k * math.pi ** (2 * k) / math.factorial(2 * k + 1) / wave_scale for k in range(6)]
 
 
 def coherence_chunk(dx, dy, dz):
@@ -55,8 +55,7 @@
     q = SIN_TERMS[4]
     for term in SIN_TERMS[3::-1]:
         q = q * f2 + term
-    scale = f * root_inv * (1.0 / (math.pi * wave_scale))
-    return sign * q * scale
+    return (sign * f) * (q * root_inv)
 
 
 def block_points(slot_ref, mode_count):
@@ -77,11 +76,11 @@
         return carry
 
     lax.fori_loop(0, length // CHUNK, chunk, 0, unroll=8)
-    shapes = slot_ref[0:mode_count, :]
+    shapes = slot_ref[0:mode_count, :] * weight.astype(jnp.bfloat16)
     product = lax.dot_general(
         tile_ref[...], shapes, (((1,), (1,)), ((), ())), preferred_element_type=jnp.float32
     )
-    out_ref[...] += weight * product
+    out_ref[...] += product
 
 
 def shift_of(j, rows):
@@ -150,7 +149,7 @@
             rowpts_ref[k, s * nodes:(s + 1) * nodes, :] = jnp.broadcast_to(column, (nodes, nodes))
 
     acc_ref[...] = jnp.zeros_like(acc_ref)
-    accumulate_block(packed_ref, 0.5, rowpts_ref, acc_ref, tile_ref, mode_count)
+    accumulate_block(packed_ref, jnp.float32(0.5), rowpts_ref, acc_ref, tile_ref, mode_count)
 
     def step(k, carry):
         transfer(k).wait_recv()

time: 134 us -> 134 us (level)
  no operation moved by 1% of the time
where the time goes in v8:
time: 134 us
  Pallas kernels  126 us (94%)
  local copies, waits for them, and re-layouts  3.38 us (3%)
  matrix products  1.89 us (1%)
  other arithmetic  1.66 us (1%)
    pallas_call x1, Pallas kernels, row_exchange(): pl.pallas_call(functools.partial(row_kernel, rows, cols, mode_count), out...  78.1 us
    pallas_call x1, Pallas kernels, all_reduce(): pl.pallas_call(functools.partial(ar_kernel, rows, cols), out_shape=jax.Sh...  48.3 us

profile of v8, /device:TPU:1, one launch (start us, length us, event | category | flops | bytes accessed | tf_op | source)
XLA Modules:
  0.0 134.0 jit_solution(888899777039562213)
XLA Ops:
  0.6 0.1 pad.3.clone
  0.7 0.7 fusion.14
  1.4 0.8 fusion.15
  2.2 0.9 maximum_maximum_fusion.packed_ref
  3.1 78.1 %shard_map.59 = f32[256,256]{1,0:T(8,128)S(1)} custom-call(bf16[272,128]{1,0:T(8,128)(2,1)S(1)} %maximum_maximum_fusion.packed_ref), custom_call_target="tpu_custom_call" | custom-call | flops 2818572288 | bytes 4194304 | tf_op jit(solution)/shard_map/pallas_call | solution.py:187
  81.2 0.0 copy-start
  81.3 0.7 reshape.12.y_ref
  82.0 48.3 %shard_map.60 = f32[16,32,128]{2,1,0:T(8,128)} custom-call(f32[16,32,128]{2,1,0:T(8,128)} %reshape.12.y_ref), custom_call_target="tpu_custom_call" | custom-call | tf_op jit(solution)/shard_map/pallas_call | solution.py:292
  130.3 1.0 reshape.13
  131.3 0.1 copy.6
  131.5 0.0 copy-done
  131.5 0.0 copy-start.1
  131.5 0.6 copy.7
  132.1 0.6 fusion.4
  132.7 0.0 copy-done.1
  132.8 1.3 fusion.2
  (2 shorter events, 0.0 us)
Async XLA Ops:
  81.2 50.2 %copy-start = (bf16[2048,256]{1,0:T(8,128)(2,1)S(1)}, bf16[2048,256]{1,0:T(8,128)(2,1)}, u32[]{:S(2)}) copy-start(bf16[2048,256]{1,0:T(8,128)(2,1)} %param.6) | copy-start | bytes 3145732
  131.5 1.3 copy-start.1

commit v9 on v8

--- a/solution.py
+++ b/solution.py
@@ -127,12 +127,12 @@
             device_id_type=pl.DeviceIdType.MESH,
         )
 
+    for k in range(half):
+        transfer(k).start()
     for s in range(cols):
         @pl.when(s != col)
         def _():
             col_copy(s, col).start()
-    for k in range(half):
-        transfer(k).start()
     for s in range(cols):
         @pl.when(s != col)
         def _():

time: 134 us -> 134 us (level)
  no operation moved by 1% of the time
where the time goes in v9:
time: 134 us
  Pallas kernels  126 us (94%)
  local copies, waits for them, and re-layouts  3.38 us (3%)
  matrix products  1.89 us (1%)
  other arithmetic  1.66 us (1%)
    pallas_call x1, Pallas kernels, row_exchange(): pl.pallas_call(functools.partial(row_kernel, rows, cols, mode_count), out...  78.1 us
    pallas_call x1, Pallas kernels, all_reduce(): pl.pallas_call(functools.partial(ar_kernel, rows, cols), out_shape=jax.Sh...  48.2 us

profile of v9, /device:TPU:1, one launch (start us, length us, event | category | flops | bytes accessed | tf_op | source)
XLA Modules:
  0.0 134.0 jit_solution(11068381673006894965)
XLA Ops:
  0.6 0.1 pad.3.clone
  0.7 0.7 fusion.14
  1.4 0.8 fusion.15
  2.2 0.9 maximum_maximum_fusion.packed_ref
  3.1 78.1 %shard_map.59 = f32[256,256]{1,0:T(8,128)S(1)} custom-call(bf16[272,128]{1,0:T(8,128)(2,1)S(1)} %maximum_maximum_fusion.packed_ref), custom_call_target="tpu_custom_call" | custom-call | flops 2818572288 | bytes 4194304 | tf_op jit(solution)/shard_map/pallas_call | solution.py:187
  81.2 0.0 copy-start
  81.2 0.7 reshape.12.y_ref
  82.0 48.2 %shard_map.60 = f32[16,32,128]{2,1,0:T(8,128)} custom-call(f32[16,32,128]{2,1,0:T(8,128)} %reshape.12.y_ref), custom_call_target="tpu_custom_call" | custom-call | tf_op jit(solution)/shard_map/pallas_call | solution.py:292
  130.2 1.0 reshape.13
  131.2 0.1 copy.6
  131.4 0.0 copy-done
  131.4 0.0 copy-start.1
  131.4 0.6 copy.7
  132.1 0.6 fusion.4
  132.7 0.0 copy-done.1
  132.7 1.3 fusion.2
  (2 shorter events, 0.0 us)
Async XLA Ops:
  81.2 50.2 %copy-start = (bf16[2048,256]{1,0:T(8,128)(2,1)S(1)}, bf16[2048,256]{1,0:T(8,128)(2,1)}, u32[]{:S(2)}) copy-start(bf16[2048,256]{1,0:T(8,128)(2,1)} %param.6) | copy-start | bytes 3145732
  131.4 1.3 copy-start.1

commit v10 on v9

--- a/solution.py
+++ b/solution.py
@@ -129,10 +129,8 @@
 
     for k in range(half):
         transfer(k).start()
-    for s in range(cols):
-        @pl.when(s != col)
-        def _():
-            col_copy(s, col).start()
+    for p in range(1, cols):
+        col_copy(lax.rem(col + p, cols), col).start()
     for s in range(cols):
         @pl.when(s != col)
         def _():
@@ -243,10 +241,9 @@
         )
 
     def exchange(src_of, dst_of, send, recv, count, me, peer_of):
-        for s in range(count):
-            @pl.when(s != me)
-            def _():
-                copy(src_of(s), dst_of(me), send, recv, s, me, peer_of(s)).start()
+        for p in range(1, count):
+            s = lax.rem(me + p, count)
+            copy(src_of(s), dst_of(me), send, recv, s, me, peer_of(s)).start()
         for s in range(count):
             @pl.when(s != me)
             def _():

time: 134 us -> 133 us (level)
    pallas_call x1, Pallas kernels: 48.2 us -> 46.5 us  [all_reduce(): pl.pallas_call(functools.partial(ar_kernel, rows, cols), out_shape=jax.Sh...]
where the time goes in v10:
time: 133 us; the launch traced here: 132 us
  Pallas kernels  125 us (94%)
  local copies, waits for them, and re-layouts  3.38 us (3%)
  matrix products  1.9 us (1%)
  other arithmetic  1.66 us (1%)
    pallas_call x1, Pallas kernels, row_exchange(): pl.pallas_call(functools.partial(row_kernel, rows, cols, mode_count), out...  78.1 us
    pallas_call x1, Pallas kernels, all_reduce(): pl.pallas_call(functools.partial(ar_kernel, rows, cols), out_shape=jax.Sh...  46.5 us

profile of v10, /device:TPU:1, one launch (start us, length us, event | category | flops | bytes accessed | tf_op | source)
XLA Modules:
  0.0 132.3 jit_solution(18020093763391817516)
XLA Ops:
  0.6 0.1 pad.3.clone
  0.7 0.7 fusion.14
  1.4 0.8 fusion.15
  2.2 0.9 maximum_maximum_fusion.packed_ref
  3.1 78.1 %shard_map.59 = f32[256,256]{1,0:T(8,128)S(1)} custom-call(bf16[272,128]{1,0:T(8,128)(2,1)S(1)} %maximum_maximum_fusion.packed_ref), custom_call_target="tpu_custom_call" | custom-call | flops 2818572288 | bytes 4194304 | tf_op jit(solution)/shard_map/pallas_call | solution.py:185
  81.2 0.0 copy-start
  81.2 0.7 reshape.12.y_ref
  82.0 46.5 %shard_map.60 = f32[16,32,128]{2,1,0:T(8,128)} custom-call(f32[16,32,128]{2,1,0:T(8,128)} %reshape.12.y_ref), custom_call_target="tpu_custom_call" | custom-call | tf_op jit(solution)/shard_map/pallas_call | solution.py:289
  128.5 1.0 reshape.13
  129.5 0.1 copy.6
  129.7 0.0 copy-done
  129.7 0.0 copy-start.1
  129.7 0.6 copy.7
  130.3 0.6 fusion.4
  131.0 0.0 copy-done.1
  131.0 1.3 fusion.2
  (2 shorter events, 0.0 us)
Async XLA Ops:
  81.2 48.4 %copy-start = (bf16[2048,256]{1,0:T(8,128)(2,1)S(1)}, bf16[2048,256]{1,0:T(8,128)(2,1)}, u32[]{:S(2)}) copy-start(bf16[2048,256]{1,0:T(8,128)(2,1)} %param.6) | copy-start | bytes 3145732
  129.7 1.3 copy-start.1

commit v11 on v10

--- a/solution.py
+++ b/solution.py
@@ -131,20 +131,21 @@
         transfer(k).start()
     for p in range(1, cols):
         col_copy(lax.rem(col + p, cols), col).start()
-    for s in range(cols):
-        @pl.when(s != col)
-        def _():
-            col_copy(s, s).wait_recv()
-
     eye = (lax.broadcasted_iota(jnp.int32, (nodes, nodes), 0)
            == lax.broadcasted_iota(jnp.int32, (nodes, nodes), 1)).astype(jnp.bfloat16)
-    own_tail = packed_ref[mode_count:mode_count + 16, :]
-    for s in range(cols):
-        tail = jnp.where(s == col, own_tail, colbuf[s, mode_count:mode_count + 16, :])
+
+    def place_points(slot, tail):
         moved = lax.dot_general(eye, tail, (((1,), (1,)), ((), ())), preferred_element_type=jnp.float32)
+        start = pl.multiple_of(slot * nodes, nodes)
         for k in range(3):
             column = moved[:, k:k + 1] * 256.0 + moved[:, k + 3:k + 4]
-            rowpts_ref[k, s * nodes:(s + 1) * nodes, :] = jnp.broadcast_to(column, (nodes, nodes))
+            rowpts_ref[k, pl.ds(start, nodes), :] = jnp.broadcast_to(column, (nodes, nodes))
+
+    place_points(col, packed_ref[mode_count:mode_count + 16, :])
+    for p in range(1, cols):
+        s = lax.rem(col + cols - p, cols)
+        col_copy(s, s).wait_recv()
+        place_points(s, colbuf[s, mode_count:mode_count + 16, :])
 
     acc_ref[...] = jnp.zeros_like(acc_ref)
     accumulate_block(packed_ref, jnp.float32(0.5), rowpts_ref, acc_ref, tile_ref, mode_count)

time: 133 us -> 133 us (level)
  no operation moved by 1% of the time
where the time goes in v11:
time: 133 us; the launch traced here: 132 us
  Pallas kernels  125 us (94%)
  local copies, waits for them, and re-layouts  3.38 us (3%)
  matrix products  1.9 us (1%)
  other arithmetic  1.66 us (1%)
    pallas_call x1, Pallas kernels, row_exchange(): pl.pallas_call(functools.partial(row_kernel, rows, cols, mode_count), out...  78.1 us
    pallas_call x1, Pallas kernels, all_reduce(): pl.pallas_call(functools.partial(ar_kernel, rows, cols), out_shape=jax.Sh...  46.7 us

profile of v11, /device:TPU:1, one launch (start us, length us, event | category | flops | bytes accessed | tf_op | source)
XLA Modules:
  0.0 132.5 jit_solution(14272710145070424669)
XLA Ops:
  0.6 0.1 pad.3.clone
  0.7 0.7 fusion.14
  1.4 0.8 fusion.15
  2.2 0.9 maximum_maximum_fusion.packed_ref
  3.1 78.1 %shard_map.59 = f32[256,256]{1,0:T(8,128)S(1)} custom-call(bf16[272,128]{1,0:T(8,128)(2,1)S(1)} %maximum_maximum_fusion.packed_ref), custom_call_target="tpu_custom_call" | custom-call | flops 2818572288 | bytes 4194304 | tf_op jit(solution)/shard_map/pallas_call | solution.py:186
  81.2 0.0 copy-start
  81.3 0.7 reshape.12.y_ref
  82.0 46.7 %shard_map.60 = f32[16,32,128]{2,1,0:T(8,128)} custom-call(f32[16,32,128]{2,1,0:T(8,128)} %reshape.12.y_ref), custom_call_target="tpu_custom_call" | custom-call | tf_op jit(solution)/shard_map/pallas_call | solution.py:290
  128.7 1.0 reshape.13
  129.7 0.1 copy.6
  129.9 0.0 copy-done
  129.9 0.0 copy-start.1
  129.9 0.6 copy.7
  130.5 0.6 fusion.4
  131.2 0.0 copy-done.1
  131.2 1.3 fusion.2
  (2 shorter events, 0.0 us)
Async XLA Ops:
  81.2 48.6 %copy-start = (bf16[2048,256]{1,0:T(8,128)(2,1)S(1)}, bf16[2048,256]{1,0:T(8,128)(2,1)}, u32[]{:S(2)}) copy-start(bf16[2048,256]{1,0:T(8,128)(2,1)} %param.6) | copy-start | bytes 3145732
  129.9 1.3 copy-start.1

commit v12 on v10

--- a/solution.py
+++ b/solution.py
@@ -88,12 +88,19 @@
     return odd * j + (1 - odd) * (rows - j)
 
 
-def row_kernel(rows, cols, mode_count, packed_ref, out_ref, recv, colbuf, rowpts_ref, tile_ref, acc_ref,
-               send_sems, recv_sems, col_send, col_recv):
+def row_kernel(rows, cols, mode_count, coords_ref, shapes_ref, out_ref, packed_ref, recv, colbuf, rowpts_ref,
+               tile_ref, acc_ref, send_sems, recv_sems, col_send, col_recv):
     me = lax.axis_index("row")
     col = lax.axis_index("col")
     half = rows // 2
     nodes = packed_ref.shape[1]
+    wide = coords_ref[...].astype(jnp.float32)
+    high = jnp.floor(wide * (1.0 / 256.0))
+    low = wide - 256.0 * high
+    packed_ref[0:mode_count, :] = shapes_ref[...]
+    packed_ref[mode_count:mode_count + 3, :] = high.astype(jnp.bfloat16)
+    packed_ref[mode_count + 3:mode_count + 6, :] = low.astype(jnp.bfloat16)
+    packed_ref[mode_count + 6:mode_count + 16, :] = jnp.zeros((10, nodes), jnp.bfloat16)
     colbuf[...] = jnp.zeros_like(colbuf)
     barrier = pltpu.get_barrier_semaphore()
     for p in range(1, rows):
@@ -176,8 +183,9 @@
             col_copy(s, col).wait_send()
 
 
-def row_exchange(packed, rows, cols, mode_count):
-    nodes = packed.shape[1]
+def row_exchange(coords, mode_shapes, rows, cols, mode_count):
+    nodes = mode_shapes.shape[1]
+    packed = jax.ShapeDtypeStruct((mode_count + 16, nodes), mode_shapes.dtype)
     length = cols * nodes
     half = rows // 2
     vmem = pltpu.MemorySpace.VMEM
@@ -185,9 +193,10 @@
     return pl.pallas_call(
         functools.partial(row_kernel, rows, cols, mode_count),
         out_shape=jax.ShapeDtypeStruct((mode_count, mode_count), jnp.float32),
-        in_specs=[pl.BlockSpec(memory_space=vmem)],
+        in_specs=[pl.BlockSpec(memory_space=vmem)] * 2,
         out_specs=pl.BlockSpec(memory_space=vmem),
         scratch_shapes=[
+            pltpu.VMEM(packed.shape, packed.dtype),
             pltpu.VMEM((half,) + packed.shape, packed.dtype),
             pltpu.VMEM((cols,) + packed.shape, packed.dtype),
             pltpu.VMEM((3, length, nodes), jnp.float32),
@@ -204,7 +213,7 @@
         cost_estimate=pl.CostEstimate(
             flops=flops, transcendentals=(half + 1) * length * nodes, bytes_accessed=4 * 1024 * 1024
         ),
-    )(packed)
+    )(coords, mode_shapes)
 
 def gather_all(block, axis, count):
     spread = jnp.broadcast_to(block[None], (count,) + block.shape)
@@ -316,8 +325,7 @@
     rows = lax.axis_size("row")
     cols = lax.axis_size("col")
     mode_count, block_nodes = mode_shapes.shape
-    packed = pack_block(coords, mode_shapes)
-    partial = row_exchange(packed, rows, cols, mode_count)
+    partial = row_exchange(coords, mode_shapes, rows, cols, mode_count)
     total = all_reduce(partial, rows, cols)
     modal_csd = total + total.T
     real_part = response_gain[0]

time: 133 us -> 132 us (level)
  other arithmetic: 1.66 us -> 0.04 us
  local copies, waits for them, and re-layouts: 3.38 us -> 4.82 us
    unnamed x5 -> x9, local copies, waits for them, and re-layouts: 0.66 us -> 2.18 us
where the time goes in v12:
time: 132 us
  Pallas kernels  125 us (95%)
  local copies, waits for them, and re-layouts  4.82 us (4%)
  matrix products  1.89 us (1%)
    pallas_call x1, Pallas kernels, row_exchange(): pl.pallas_call(functools.partial(row_kernel, rows, cols, mode_count), out...  78.1 us
    pallas_call x1, Pallas kernels, all_reduce(): pl.pallas_call(functools.partial(ar_kernel, rows, cols), out_shape=jax.Sh...  46.5 us

profile of v12, /device:TPU:1, one launch (start us, length us, event | category | flops | bytes accessed | tf_op | source)
XLA Modules:
  0.0 132.0 jit_solution(6976028253321998026)
XLA Ops:
  0.6 0.8 fusion.14
  1.4 0.0 copy-start
  1.4 0.8 copy-done
  2.2 0.0 copy-start.1
  2.2 0.7 copy-done.1
  2.9 78.1 %shard_map.59 = f32[256,256]{1,0:T(8,128)S(1)} custom-call(s32[3,128]{1,0:T(4,128)S(1)} %copy-done.1, bf16[256,128]{1,0:T(8,128)(2,1)S(1)} %copy-done), custom_call_target="tpu_custom_call" | custom-call | flops 2818572288 | bytes 4194304 | tf_op jit(solution)/shard_map/pallas_call | solution.py:193
  81.0 0.0 copy-start.2
  81.1 0.7 reshape.12.y_ref
  81.8 46.5 %shard_map.60 = f32[16,32,128]{2,1,0:T(8,128)} custom-call(f32[16,32,128]{2,1,0:T(8,128)} %reshape.12.y_ref), custom_call_target="tpu_custom_call" | custom-call | tf_op jit(solution)/shard_map/pallas_call | solution.py:298
  128.3 1.0 reshape.13
  129.3 0.1 copy.6
  129.5 0.0 copy-done.2
  129.5 0.0 copy-start.3
  129.5 0.6 copy.7
  130.1 0.6 fusion.4
  130.7 0.0 copy-done.3
  130.8 1.3 fusion.2
  (1 shorter events, 0.0 us)
Async XLA Ops:
  1.4 0.8 copy-start
  2.2 0.7 copy-start.1
  81.0 48.4 %copy-start.2 = (bf16[2048,256]{1,0:T(8,128)(2,1)S(1)}, bf16[2048,256]{1,0:T(8,128)(2,1)}, u32[]{:S(2)}) copy-start(bf16[2048,256]{1,0:T(8,128)(2,1)} %param.6) | copy-start | bytes 3145732
  129.5 1.3 copy-start.3

commit v13 on v10

--- a/solution.py
+++ b/solution.py
@@ -326,8 +326,9 @@
         real_part[:, None] * real_part[None, :] + imag_part[:, None] * imag_part[None, :]
     ) * modal_csd
     weighted_high, weighted_low = split_parts(weighted)
-    mapped = jnp.dot(output_shapes, weighted_high, preferred_element_type=jnp.float32)
-    mapped = mapped + jnp.dot(output_shapes, weighted_low, preferred_element_type=jnp.float32)
+    both = jnp.dot(output_shapes, jnp.concatenate([weighted_high, weighted_low], axis=1),
+                   preferred_element_type=jnp.float32)
+    mapped = both[:, :mode_count] + both[:, mode_count:]
     response_power = jnp.sum(mapped * output_shapes.astype(jnp.float32), axis=1)
     return (response_power, modal_csd)
 

time: 133 us -> 136 us (1.023)
  other arithmetic: 1.66 us -> 5.19 us
    reduce_sum x0 -> x1, other arithmetic: none -> 3.29 us  [local(): response_power = jnp.sum(mapped * output_shapes.astype(jnp.float32), axis=1)]
    dot_general x2 -> x1, matrix products: 1.9 us -> 2.72 us  [local(): jnp.dot(output_shapes, jnp.concatenate([weighted_high, weighted_low], axi...]
where the time goes in v13:
time: 136 us
  Pallas kernels  125 us (92%)
  other arithmetic  5.19 us (4%)
  matrix products  2.72 us (2%)
  local copies, waits for them, and re-layouts  2.62 us (2%)
    pallas_call x1, Pallas kernels, row_exchange(): pl.pallas_call(functools.partial(row_kernel, rows, cols, mode_count), out...  78.1 us
    pallas_call x1, Pallas kernels, all_reduce(): pl.pallas_call(functools.partial(ar_kernel, rows, cols), out_shape=jax.Sh...  46.5 us
    reduce_sum x1, other arithmetic, local(): response_power = jnp.sum(mapped * output_shapes.astype(jnp.float32), axis=1)  3.29 us
    dot_general x1, matrix products, local(): jnp.dot(output_shapes, jnp.concatenate([weighted_high, weighted_low], axi...  2.72 us

profile of v13, /device:TPU:1, one launch (start us, length us, event | category | flops | bytes accessed | tf_op | source)
XLA Modules:
  0.0 135.9 jit_solution(9616742807226262704)
XLA Ops:
  0.6 0.7 fusion.6
  1.3 0.1 pad.5.clone
  1.4 0.9 maximum_maximum_fusion.packed_ref
  2.3 78.1 %shard_map.59 = f32[256,256]{1,0:T(8,128)S(1)} custom-call(bf16[272,128]{1,0:T(8,128)(2,1)S(1)} %maximum_maximum_fusion.packed_ref), custom_call_target="tpu_custom_call" | custom-call | flops 2818572288 | bytes 4194304 | tf_op jit(solution)/shard_map/pallas_call | solution.py:185
  80.5 0.0 copy-start.2
  80.5 0.0 copy-start
  80.5 0.7 reshape.12.y_ref
  81.2 46.5 %shard_map.60 = f32[16,32,128]{2,1,0:T(8,128)} custom-call(f32[16,32,128]{2,1,0:T(8,128)} %reshape.12.y_ref), custom_call_target="tpu_custom_call" | custom-call | tf_op jit(solution)/shard_map/pallas_call | solution.py:289
  127.7 1.0 reshape.13
  128.7 0.1 copy.6
  128.9 0.0 copy-done.2
  128.9 0.1 fusion.5
  129.0 0.0 copy-start.1
  129.1 0.1 subtract_convert_fusion
  129.2 0.0 copy-done
  129.2 2.7 %convolution_bitcast_fusion = f32[2048,512]{0,1:T(8,128)} fusion(bf16[2048,256]{1,0:T(8,128)(2,1)S(1)} %copy-done, bf16[256,256]{1,0:T(8,128)(2,1)S(1)} %subtract_convert_fusion, bf16[256,256]{1,0:T(8,128)(2,1)S(1)} %get-tuple-element.2), kind=kOutput, calls=%fused_computation | convolution fusion | flops 537395200 | bytes 5505024 | tf_op jit(solution)/shard_map/dot_general | solution.py:329
  131.9 0.0 copy-done.1
  131.9 0.6 copy.7
  132.6 3.3 %fusion.1 = f32[2048]{0:T(1024)} fusion(f32[2048,512]{0,1:T(8,128)} %convolution_bitcast_fusion, bf16[2048,256]{0,1:T(8,128)(2,1)S(1)} %copy.7), kind=kLoop, calls=%fused_computation.3 | loop fusion | flops 2095104 | bytes 5251072 | tf_op jit(solution)/shard_map/reduce_sum | solution.py:332
  (2 shorter events, 0.0 us)
Async XLA Ops:
  80.5 48.4 %copy-start.2 = (f32[2,256]{1,0:T(2,128)S(1)}, f32[2,256]{1,0:T(2,128)}, u32[]{:S(2)}) copy-start(f32[2,256]{1,0:T(2,128)} %param.7) | copy-start | bytes 6148
  80.5 48.7 %copy-start = (bf16[2048,256]{1,0:T(8,128)(2,1)S(1)}, bf16[2048,256]{1,0:T(8,128)(2,1)}, u32[]{:S(2)}) copy-start(bf16[2048,256]{1,0:T(8,128)(2,1)} %param.6) | copy-start | bytes 3145732
  129.0 2.9 %copy-start.1 = (f32[256,256]{1,0:T(8,128)}, f32[256,256]{1,0:T(8,128)S(1)}, u32[]{:S(2)}) copy-start(f32[256,256]{1,0:T(8,128)S(1)} %get-tuple-element.3) | copy-start | bytes 786436

commit v14 on v10

--- a/solution.py
+++ b/solution.py
@@ -38,7 +38,7 @@
     return high * 256.0 + low
 
 
-CHUNK = 32
+CHUNK = 64
 SIN_TERMS = [(-1) ** k * math.pi ** (2 * k) / math.factorial(2 * k + 1) / wave_scale for k in range(6)]
 
 
@@ -75,7 +75,7 @@
         tile_ref[pl.ds(r0, CHUNK), :] = coherence_chunk(dx, dy, dz).astype(jnp.bfloat16)
         return carry
 
-    lax.fori_loop(0, length // CHUNK, chunk, 0, unroll=8)
+    lax.fori_loop(0, length // CHUNK, chunk, 0, unroll=4)
     shapes = slot_ref[0:mode_count, :] * weight.astype(jnp.bfloat16)
     product = lax.dot_general(
         tile_ref[...], shapes, (((1,), (1,)), ((), ())), preferred_element_type=jnp.float32

time: 133 us -> 133 us (level)
  no operation moved by 1% of the time
where the time goes in v14:
time: 133 us; the launch traced here: 132 us
  Pallas kernels  125 us (94%)
  local copies, waits for them, and re-layouts  3.38 us (3%)
  matrix products  1.89 us (1%)
  other arithmetic  1.66 us (1%)
    pallas_call x1, Pallas kernels, row_exchange(): pl.pallas_call(functools.partial(row_kernel, rows, cols, mode_count), out...  78.1 us
    pallas_call x1, Pallas kernels, all_reduce(): pl.pallas_call(functools.partial(ar_kernel, rows, cols), out_shape=jax.Sh...  46.5 us

profile of v14, /device:TPU:1, one launch (start us, length us, event | category | flops | bytes accessed | tf_op | source)
XLA Modules:
  0.0 132.3 jit_solution(10082311157122222761)
XLA Ops:
  0.6 0.1 pad.3.clone
  0.7 0.7 fusion.14
  1.4 0.8 fusion.15
  2.2 0.9 maximum_maximum_fusion.packed_ref
  3.1 78.1 %shard_map.59 = f32[256,256]{1,0:T(8,128)S(1)} custom-call(bf16[272,128]{1,0:T(8,128)(2,1)S(1)} %maximum_maximum_fusion.packed_ref), custom_call_target="tpu_custom_call" | custom-call | flops 2818572288 | bytes 4194304 | tf_op jit(solution)/shard_map/pallas_call | solution.py:185
  81.2 0.0 copy-start
  81.2 0.7 reshape.12.y_ref
  82.0 46.5 %shard_map.60 = f32[16,32,128]{2,1,0:T(8,128)} custom-call(f32[16,32,128]{2,1,0:T(8,128)} %reshape.12.y_ref), custom_call_target="tpu_custom_call" | custom-call | tf_op jit(solution)/shard_map/pallas_call | solution.py:289
  128.5 1.0 reshape.13
  129.5 0.1 copy.6
  129.7 0.0 copy-done
  129.7 0.0 copy-start.1
  129.7 0.6 copy.7
  130.4 0.6 fusion.4
  131.0 0.0 copy-done.1
  131.0 1.3 fusion.2
  (2 shorter events, 0.0 us)
Async XLA Ops:
  81.2 48.5 %copy-start = (bf16[2048,256]{1,0:T(8,128)(2,1)S(1)}, bf16[2048,256]{1,0:T(8,128)(2,1)}, u32[]{:S(2)}) copy-start(bf16[2048,256]{1,0:T(8,128)(2,1)} %param.6) | copy-start | bytes 3145732
  129.7 1.3 copy-start.1

commit v15 on v10

--- a/solution.py
+++ b/solution.py
@@ -75,7 +75,7 @@
         tile_ref[pl.ds(r0, CHUNK), :] = coherence_chunk(dx, dy, dz).astype(jnp.bfloat16)
         return carry
 
-    lax.fori_loop(0, length // CHUNK, chunk, 0, unroll=8)
+    lax.fori_loop(0, length // CHUNK, chunk, 0, unroll=16)
     shapes = slot_ref[0:mode_count, :] * weight.astype(jnp.bfloat16)
     product = lax.dot_general(
         tile_ref[...], shapes, (((1,), (1,)), ((), ())), preferred_element_type=jnp.float32

time: 133 us -> 132 us (level)
  no operation moved by 1% of the time
where the time goes in v15:
time: 132 us
  Pallas kernels  124 us (94%)
  local copies, waits for them, and re-layouts  3.38 us (3%)
  matrix products  1.9 us (1%)
  other arithmetic  1.66 us (1%)
    pallas_call x1, Pallas kernels, row_exchange(): pl.pallas_call(functools.partial(row_kernel, rows, cols, mode_count), out...  78.1 us
    pallas_call x1, Pallas kernels, all_reduce(): pl.pallas_call(functools.partial(ar_kernel, rows, cols), out_shape=jax.Sh...  46.4 us

profile of v15, /device:TPU:1, one launch (start us, length us, event | category | flops | bytes accessed | tf_op | source)
XLA Modules:
  0.0 132.1 jit_solution(12886814052450800754)
XLA Ops:
  0.6 0.1 pad.3.clone
  0.7 0.7 fusion.14
  1.4 0.8 fusion.15
  2.2 0.9 maximum_maximum_fusion.packed_ref
  3.1 78.1 %shard_map.59 = f32[256,256]{1,0:T(8,128)S(1)} custom-call(bf16[272,128]{1,0:T(8,128)(2,1)S(1)} %maximum_maximum_fusion.packed_ref), custom_call_target="tpu_custom_call" | custom-call | flops 2818572288 | bytes 4194304 | tf_op jit(solution)/shard_map/pallas_call | solution.py:185
  81.2 0.0 copy-start
  81.2 0.7 reshape.12.y_ref
  81.9 46.4 %shard_map.60 = f32[16,32,128]{2,1,0:T(8,128)} custom-call(f32[16,32,128]{2,1,0:T(8,128)} %reshape.12.y_ref), custom_call_target="tpu_custom_call" | custom-call | tf_op jit(solution)/shard_map/pallas_call | solution.py:289
  128.3 1.0 reshape.13
  129.3 0.1 copy.6
  129.5 0.0 copy-done
  129.5 0.0 copy-start.1
  129.5 0.6 copy.7
  130.2 0.6 fusion.4
  130.8 0.0 copy-done.1
  130.8 1.3 fusion.2
  (2 shorter events, 0.0 us)
Async XLA Ops:
  81.2 48.3 %copy-start = (bf16[2048,256]{1,0:T(8,128)(2,1)S(1)}, bf16[2048,256]{1,0:T(8,128)(2,1)}, u32[]{:S(2)}) copy-start(bf16[2048,256]{1,0:T(8,128)(2,1)} %param.6) | copy-start | bytes 3145732
  129.5 1.3 copy-start.1
